TPU v7x, 32 devices: a whole 2x2x4 slice. The times are simulated.
32 devices in a mesh: ctx: 8 (over z, x), head: 4 (over y, core).
Axes of the slice: x: 2, y: 2, z: 4, core: 2. Of those that a mesh axis runs over, the one named last changes fastest.
Arguments:
- q_nope: bfloat16 [1024, 4096], P('ctx', 'head'), may hold values from -6 to 6
- q_rope: bfloat16 [1024, 2048], P('ctx', 'head'), may hold values from -300 to 300
- latent: bfloat16 [1024, 512], P('ctx'), may hold values from -6 to 6
- k_rope: bfloat16 [1024, 64], P('ctx'), may hold values from -4 to 4
- span_order: int32 [16], replicated, may hold values from 0 to 15, each once
- w_uk: bfloat16 [512, 4096], P(None, 'head'), may hold values from -0.25 to 0.25
- w_uv: bfloat16 [512, 4096], P(None, 'head'), may hold values from -0.25 to 0.25
- w_o: bfloat16 [4096, 7168], P('head', 'ctx'), may hold values from -0.125 to 0.125
Outputs:
- attended: bfloat16 [1024, 7168], P('ctx', 'head')
Inputs may be any that keep to these rules, and one draw needn't show every extreme that they name: `span_order`: a permutation of 0 to 15.
All inputs are finite; a program needn't handle non-finite values.
Results may differ from a plain program's by a relative error of at most 0.014.
Values may be sent and summed in bfloat16 or wider, within the bound.
No kernel may reach another device: no remote copies, remote signals or barrier semaphores. Data moves between devices by JAX's collectives and lax.ppermute only.
A program may use at most 128 MiB of HBM per device.

v0:
```python
import math
import jax
import jax.numpy as jnp
from jax import lax
from jax.sharding import PartitionSpec as P

LAT = 512
ROPE = 64
NOPE = 128
VDIM = 128


def span_place(slot_ids, table):
    match = slot_ids[:, None] == jnp.arange(table.shape[0], dtype=jnp.int32)[None, :]
    return jnp.sum(jnp.where(match, table[None, :], 0), axis=1)


def local(q_nope, q_rope, latent, k_rope, span_order, w_uk, w_uv, w_o):
    rows = q_nope.shape[0]
    half = rows // 2
    heads = w_uk.shape[1] // NOPE
    scale = 1.0 / math.sqrt(NOPE + ROPE)
    local_rows = jnp.arange(rows, dtype=jnp.int32)
    query_slot = lax.axis_index("ctx") * 2 + local_rows // half
    qpos = span_place(query_slot, span_order) * half + local_rows % half
    absorbed = jnp.einsum(
        "thn,lhn->htl",
        q_nope.reshape(rows, heads, NOPE),
        w_uk.reshape(LAT, heads, NOPE),
        preferred_element_type=jnp.float32,
    ).astype(jnp.bfloat16)
    rotary = q_rope.reshape(rows, heads, ROPE)
    lat_piece = lax.all_gather(latent, "ctx", axis=0, tiled=True)
    rope_piece = lax.all_gather(k_rope, "ctx", axis=0, tiled=True)
    count = lat_piece.shape[0]
    key_rows = jnp.arange(count, dtype=jnp.int32)
    kpos = span_place(key_rows // half, span_order) * half + key_rows % half
    running = jnp.full((heads, rows), -1e30, jnp.float32)
    score = jnp.einsum("htl,kl->htk", absorbed, lat_piece, preferred_element_type=jnp.float32)
    score = score + jnp.einsum(
        "thr,kr->htk", rotary, rope_piece, preferred_element_type=jnp.float32
    )
    score = score * scale
    visible = kpos[None, None, :] <= qpos[None, :, None]
    newest = jnp.maximum(running, jnp.max(jnp.where(visible, score, -1e30), axis=-1))
    weight = jnp.where(visible, jnp.exp(score - newest[..., None]), 0.0)
    summed = jnp.sum(weight, axis=-1)
    accum = jnp.einsum(
        "htk,kl->htl", weight.astype(jnp.bfloat16), lat_piece, preferred_element_type=jnp.float32
    )
    running, summed, accum = (newest, summed, accum)
    context = (accum / summed[..., None]).astype(jnp.bfloat16)
    heads_out = jnp.einsum(
        "htl,lhv->thv", context, w_uv.reshape(LAT, heads, VDIM), preferred_element_type=jnp.float32
    ).astype(jnp.bfloat16)
    heads_out = heads_out.reshape(rows, heads * VDIM)
    every_token = jnp.dot(
        lax.all_gather(heads_out, "ctx", axis=0, tiled=True),
        w_o,
        preferred_element_type=jnp.float32,
    ).astype(jnp.bfloat16)
    partial_value = lax.all_to_all(every_token, "ctx", split_axis=0, concat_axis=1, tiled=True)
    return (
        lax.psum_scatter(partial_value, "head", scatter_dimension=1, tiled=True)
        .astype(jnp.float32)
        .astype(jnp.bfloat16)
    )


def solution(mesh):
    placed = (
        P("ctx", "head"),
        P("ctx", "head"),
        P("ctx", None),
        P("ctx", None),
        P(),
        P(None, "head"),
        P(None, "head"),
        P("head", "ctx"),
    )
    return jax.shard_map(
        local, mesh=mesh, in_specs=placed, out_specs=P("ctx", "head"), check_vma=False
    )
```

profile of v0, /device:TPU:0, one launch (start us, length us, event | category | flops | bytes accessed | tf_op | source)
XLA Modules:
  0.0 204.4 jit_solution(16470658505095125386)
XLA Ops:
  6.5 0.0 copy-start
  6.5 0.0 all-gather.3.cloned.1.call-start
  6.5 0.7 all-gather.3.cloned.1.call-update
  7.3 0.0 all-gather.5.cloned.1.call-start
  7.3 1.0 copy.19
  8.3 2.3 %copy.24 = bf16[512,1024]{0,1:T(8,128)(2,1)} copy(bf16[512,1024]{1,0:T(8,128)(2,1)} %param.14) | data formatting | bytes 2097152 | tf_op jit(solution)/shard_map/reshape | solution.py:54
  10.6 28.3 %all_gather.10 = bf16[1024,64]{0,1:T(8,128)(2,1)S(1)} all-gather(bf16[128,64]{0,1:T(8,128)(2,1)} %param.11), channel_id=1, replica_groups=mesh['ctx'=8,'head'=4] {'ctx'}, dimensions={0}, use_global_device_ids=true | all-gather | bytes 147456 | tf_op jit(solution)/shard_map/all_gather | solution.py:34
  39.0 0.7 select_reduce_fusion.2
  39.7 0.7 select_reduce_fusion.1
  40.5 0.1 broadcast_compare_fusion
  40.6 12.1 %all-gather.3.cloned.1.call-done = bf16[1024,512]{1,0:T(8,128)(2,1)} async-done(((bf16[128,512]{1,0:T(8,128)(2,1)}), bf16[1024,512]{1,0:T(8,128)(2,1)}) %all-gather.3.cloned.1.call-update) | async-done | bytes 1048592 | tf_op jit(solution)/shard_map/all_gather | solution.py:33
  52.8 5.1 %fusion.8 = f32[8,128,1024]{2,1,0:T(8,128)} fusion(bf16[1024,512]{1,0:T(8,128)(2,1)} %all-gather.3.cloned.1.call-done, bf16[512,1024]{1,0:T(8,128)(2,1)} %param.13, bf16[128,1024]{1,0:T(8,128)(2,1)} %param.8), kind=kOutput, calls=%fused_computation.13 | convolution fusion | flops 1208483840 | bytes 6553600 | tf_op jit(solution)/shard_map/htl,kl->htk/dot_general | solution.py:39
  57.9 3.3 %select_reduce_fusion = (f32[8,128]{1,0:T(8,128)S(1)}, f32[8,128,1024]{2,1,0:T(8,128)S(1)}) fusion(pred[128,1024]{1,0:T(8,128)(4,1)S(1)} %broadcast_compare_fusion, f32[8,128,1024]{2,1,0:T(8,128)} %fusion.8, bf16[128,8,64]{0,2,1:T(8,128)(2,1)S(1)} %bitcast.53, bf16[1024,64]{0,1:T(8,128)(2,1)S(1)} %all_gather.10), kind=kOutput, calls=%fused_computation.3 | convolution fusion | flops 138411008 | bytes 8785920 | tf_op jit(solution)/shard_map/thr,kr->htk/dot_general | solution.py:40
  61.2 0.0 copy-start.1
  61.2 0.0 copy-start.2
  61.2 1.9 copy-done.1
  63.1 1.1 fusion.1
  64.3 0.0 copy-done.2
  64.3 4.8 %convolution_convert_fusion.2 = bf16[8,128,128]{1,2,0:T(8,128)(2,1)} fusion(bf16[512,8,128]{0,2,1:T(8,128)(2,1)} %bitcast.52, f32[8,128]{1,0:T(8,128)S(1)} %fusion.1, f32[8,128,1024]{2,1,0:T(8,128)} %copy-done.1, f32[8,128]{1,0:T(8,128)S(1)} %broadcast_maximum_fusion, pred[128,1024]{1,0:T(8,128)(4,1)S(1)} %broadcast_compare_fusion, ...), kind=kOutput, calls=%fused_computation.14 | convolution fusion | flops 1212284928 | bytes 6692864 | tf_op jit(solution)/shard_map/htl,lhv->thv/dot_general | solution.py:53
  69.1 0.0 all-gather.5.cloned.1.call-update
  69.1 0.0 reduce-scatter.2.cloned.1.call-start
  69.1 49.2 %all-gather.5.cloned.1.call-done = bf16[1024,1024]{0,1:T(8,128)(2,1)} async-done(((bf16[128,1024]{0,1:T(8,128)(2,1)}), bf16[1024,1024]{0,1:T(8,128)(2,1)}) %all-gather.5.cloned.1.call-update) | async-done | bytes 2097168 | tf_op jit(solution)/shard_map/all_gather | solution.py:58
  118.3 0.0 copy-done
  118.3 4.0 %convolution_convert_fusion = bf16[1024,896]{1,0:T(8,128)(2,1)S(1)} fusion(bf16[1024,1024]{0,1:T(8,128)(2,1)} %all-gather.5.cloned.1.call-done, bf16[1024,896]{1,0:T(8,128)(2,1)S(1)} %copy-done), kind=kOutput, calls=%fused_computation.11 | convolution fusion | flops 1879965696 | bytes 5767168 | tf_op jit(solution)/shard_map/dot_general | solution.py:57
  122.3 45.3 %all_to_all.19 = bf16[8,128,896]{2,1,0:T(8,128)(2,1)S(1)} all-to-all(bf16[8,128,896]{2,1,0:T(8,128)(2,1)S(1)} %bitcast.51), channel_id=1, replica_groups=mesh['ctx'=8,'head'=4] {'ctx'}, dimensions={0} | all-to-all | bytes 3670016 | tf_op jit(solution)/shard_map/all_to_all | solution.py:62
  167.5 1.5 copy.27
  169.1 0.0 reduce-scatter.2.cloned.1.call-update
  169.1 28.8 %reduce-scatter.2.cloned.1.call-done = bf16[128,1792]{1,0:T(8,128)(2,1)} async-done(((bf16[128,7168]{1,0:T(8,128)(2,1)}), bf16[128,1792]{1,0:T(8,128)(2,1)}) %reduce-scatter.2.cloned.1.call-update) | async-done | bytes 458768 | tf_op jit(solution)/shard_map/reduce_scatter | solution.py:64
  (5 shorter events, 0.0 us)
Async XLA Ops:
  6.5 111.8 %copy-start = (bf16[1024,896]{1,0:T(8,128)(2,1)S(1)}, bf16[1024,896]{1,0:T(8,128)(2,1)}, u32[]{:S(2)}) copy-start(bf16[1024,896]{1,0:T(8,128)(2,1)} %param.15) | copy-start | bytes 5505028
  6.5 46.2 %all-gather.3.cloned.1.call-start = ((), (), s32[]{:S(2)}) async-start(), calls=%async_computation.2 | async-start | bytes 1179648 | tf_op jit(solution)/shard_map/all_gather | solution.py:33
  7.3 111.0 %all-gather.5.cloned.1.call-start = ((), (), s32[]{:S(2)}) async-start(), calls=%async_computation.3 | async-start | bytes 2359296 | tf_op jit(solution)/shard_map/all_gather | solution.py:58
  61.2 1.9 copy-start.1
  61.2 3.0 %copy-start.2 = (bf16[1024,512]{1,0:T(8,128)(2,1)S(1)}, bf16[1024,512]{1,0:T(8,128)(2,1)}, u32[]{:S(2)}) copy-start(bf16[1024,512]{1,0:T(8,128)(2,1)} %all-gather.3.cloned.1.call-done) | copy-start | bytes 3145732
  69.1 128.8 %reduce-scatter.2.cloned.1.call-start = ((), (), s32[]{:S(2)}) async-start(), calls=%async_computation.4 | async-start | bytes 2293760 | tf_op jit(solution)/shard_map/reduce_scatter | solution.py:64
Sparse Core Ops, SparseCore 0:
  9.5 43.2 all-gather.2
  69.2 49.0 all-gather.4
  169.2 28.5 reduce-scatter.1
where the time goes:
time: 205 us; the launch traced here: 204 us
  waiting for transfers between devices  90.8 us (44%)
  blocking collectives  73.6 us (36%)
  matrix products  17.2 us (8%)
  between operations  13.2 us (6%)
  local copies, waits for them, and re-layouts  6.76 us (3%)
  other arithmetic  2.76 us (1%)
    all_gather x1, waiting for transfers between devices, local(): lax.all_gather(heads_out, 'ctx', axis=0, tiled=True)  49.2 us
    all_to_all x1, blocking collectives, local(): lax.all_to_all(every_token, 'ctx', split_axis=0, concat_axis=1, tiled=True)  45.3 us
    reduce_scatter x1, waiting for transfers between devices, local(): lax.psum_scatter(partial_value, 'head', scatter_dimension=1, tiled=True)  28.8 us
    all_gather x1, blocking collectives, local(): rope_piece = lax.all_gather(k_rope, 'ctx', axis=0, tiled=True)  28.3 us
    all_gather x1, waiting for transfers between devices, local(): lat_piece = lax.all_gather(latent, 'ctx', axis=0, tiled=True)  12.1 us
    dot_general x1, matrix products, local(): jnp.einsum('htl,kl->htk', absorbed, lat_piece, preferred_element_type=jnp...  5.13 us
    dot_general x1, matrix products, local(): jnp.einsum('htl,lhv->thv', context, w_uv.reshape(LAT, heads, VDIM), prefe...  4.77 us
  transfers between devices with their start and end apart: 3, of which 3 were waited for; matrix products, arithmetic and copies ran while one was open for 2% of the time, Pallas kernels for 0%

commit v1 on v0

--- a/solution.py
+++ b/solution.py
@@ -8,6 +8,30 @@
 ROPE = 64
 NOPE = 128
 VDIM = 128
+
+
+def ring_apply(x, axis, dim, work, out_dim):
+    count, place, extent = (lax.axis_size(axis), lax.axis_index(axis), x.shape[dim])
+    right = [(i, (i + 1) % count) for i in range(count)]
+    left = [(b, a) for a, b in right]
+    lower, upper = (lax.ppermute(x, axis, right), lax.ppermute(x, axis, left))
+    made = work(x, place * extent)
+    length = made.shape[out_dim]
+    out = jnp.zeros((*made.shape[:out_dim], count * length, *made.shape[out_dim + 1 :]), made.dtype)
+
+    def put(out, made, owner):
+        return lax.dynamic_update_slice_in_dim(out, made, owner * length, axis=out_dim)
+
+    out = put(out, made, place)
+    for step in range(1, count // 2 + 1):
+        below, above = ((place - step) % count, (place + step) % count)
+        held = (lower, upper)
+        if step < count // 2:
+            lower, upper = (lax.ppermute(lower, axis, right), lax.ppermute(upper, axis, left))
+        out = put(out, work(held[0], below * extent), below)
+        if 2 * step < count:
+            out = put(out, work(held[1], above * extent), above)
+    return out
 
 
 def span_place(slot_ids, table):
@@ -31,14 +55,19 @@
     ).astype(jnp.bfloat16)
     rotary = q_rope.reshape(rows, heads, ROPE)
     lat_piece = lax.all_gather(latent, "ctx", axis=0, tiled=True)
-    rope_piece = lax.all_gather(k_rope, "ctx", axis=0, tiled=True)
     count = lat_piece.shape[0]
     key_rows = jnp.arange(count, dtype=jnp.int32)
     kpos = span_place(key_rows // half, span_order) * half + key_rows % half
     running = jnp.full((heads, rows), -1e30, jnp.float32)
     score = jnp.einsum("htl,kl->htk", absorbed, lat_piece, preferred_element_type=jnp.float32)
-    score = score + jnp.einsum(
-        "thr,kr->htk", rotary, rope_piece, preferred_element_type=jnp.float32
+    score = score + ring_apply(
+        k_rope,
+        "ctx",
+        0,
+        lambda shard, start: jnp.einsum(
+            "thr,kr->htk", rotary, shard, preferred_element_type=jnp.float32
+        ),
+        2,
     )
     score = score * scale
     visible = kpos[None, None, :] <= qpos[None, :, None]

time: 205 us -> 203 us (level)
  blocking collectives: 73.6 us -> 45.3 us
  starting transfers between devices: 0.08 us -> 15.6 us
  matrix products: 17.2 us -> 24 us
  other arithmetic: 2.76 us -> 4.93 us
    all_gather x1 -> x0, blocking collectives: 28.3 us -> none  [local(): rope_piece = lax.all_gather(k_rope, 'ctx', axis=0, tiled=True)]
    ppermute x0 -> x7, starting transfers between devices: none -> 15.5 us  [the longest x2 9.43 us: ring_apply(): lax.ppermute(upper, axis, left)]
    dot_general x1 -> x8, matrix products: 3.33 us -> 8.98 us  [local(): jnp.einsum('thr,kr->htk', rotary, shard, preferred_element_type=jnp.float32)]
    ppermute x0 -> x7, waiting for transfers between devices: none -> 4.39 us  [the longest x3 4.38 us: ring_apply(): lax.ppermute(lower, axis, right)]
    all_gather x1, waiting for transfers between devices: 12.1 us -> 9.61 us  [local(): lat_piece = lax.all_gather(latent, 'ctx', axis=0, tiled=True)]
    broadcast_in_dim x0 -> x1, local copies, waits for them, and re-layouts: none -> 2.51 us  [ring_apply(): jnp.zeros((*made.shape[:out_dim], count * length, *made.shape[out_dim + 1...]
    reduce_sum x1, other arithmetic: 1.11 us -> 3.29 us  [local(): summed = jnp.sum(weight, axis=-1)]
  transfers between devices with their start and end apart: 3 -> 10, of which waited for: 3 -> 4; matrix products, arithmetic and copies ran while one was open for 2% -> 8% of each run, Pallas kernels for 0% -> 0%
where the time goes in v1:
time: 203 us; the launch traced here: 202 us
  waiting for transfers between devices  91.8 us (45%)
  blocking collectives  45.3 us (22%)
  matrix products  24 us (12%)
  starting transfers between devices  15.6 us (8%)
  between operations  13.3 us (7%)
  local copies, waits for them, and re-layouts  7.35 us (4%)
  other arithmetic  4.93 us (2%)
    all_gather x1, waiting for transfers between devices, local(): lax.all_gather(heads_out, 'ctx', axis=0, tiled=True)  49 us
    all_to_all x1, blocking collectives, local(): lax.all_to_all(every_token, 'ctx', split_axis=0, concat_axis=1, tiled=True)  45.3 us
    reduce_scatter x1, waiting for transfers between devices, local(): lax.psum_scatter(partial_value, 'head', scatter_dimension=1, tiled=True)  28.8 us
    all_gather x1, waiting for transfers between devices, local(): lat_piece = lax.all_gather(latent, 'ctx', axis=0, tiled=True)  9.61 us
    ppermute x2, starting transfers between devices, ring_apply(): lax.ppermute(upper, axis, left)  9.43 us
    dot_general x8, matrix products, local(): jnp.einsum('thr,kr->htk', rotary, shard, preferred_element_type=jnp.float32)  8.98 us
    dot_general x1, matrix products, local(): jnp.einsum('htl,kl->htk', absorbed, lat_piece, preferred_element_type=jnp...  6.31 us
    ppermute x2, starting transfers between devices, ring_apply(): lower, upper = (lax.ppermute(x, axis, right), lax.ppermute(x, axis, left))  6.07 us
  transfers between devices with their start and end apart: 10, of which 4 were waited for; matrix products, arithmetic and copies ran while one was open for 8% of the time, Pallas kernels for 0%

profile of v1, /device:TPU:0, one launch (start us, length us, event | category | flops | bytes accessed | tf_op | source)
XLA Modules:
  0.0 202.3 jit_solution(3432561324719994275)
XLA Ops:
  6.5 3.0 %collective-permute-start = (bf16[128,64]{0,1:T(8,128)(2,1)}, bf16[128,64]{0,1:T(8,128)(2,1)S(1)}, u32[]{:S(2)}, u32[]{:S(2)}) collective-permute-start(bf16[128,64]{0,1:T(8,128)(2,1)} %param.11), channel_id=1, source_target_pairs={{0,4},{4,8},{8,12},{12,16},{16,20},{20,24},{24,28},{28,0},{1,5},{5... | collective-permute-start | bytes 49160 | tf_op jit(solution)/shard_map/ppermute | solution.py:17
  9.5 3.1 %collective-permute-start.1 = (bf16[128,64]{0,1:T(8,128)(2,1)}, bf16[128,64]{0,1:T(8,128)(2,1)S(1)}, u32[]{:S(2)}, u32[]{:S(2)}) collective-permute-start(bf16[128,64]{0,1:T(8,128)(2,1)} %param.11), channel_id=1, source_target_pairs={{4,0},{8,4},{12,8},{16,12},{20,16},{24,20},{28,24},{0,28},{5,1},{9... | collective-permute-start | bytes 49160 | tf_op jit(solution)/shard_map/ppermute | solution.py:17
  12.6 0.0 all-gather.3.cloned.1.call-update
  12.6 0.0 all-gather.5.cloned.1.call-start
  12.7 1.0 copy.40
  13.7 0.7 select_reduce_fusion.2
  14.5 0.7 select_reduce_fusion.1
  15.2 2.5 %broadcast_in_dim.61 = f32[8,128,1024]{2,1,0:T(8,128)} broadcast(f32[]{:T(128)} %constant.111.clone.1), dimensions={} | broadcast | bytes 4194308 | tf_op jit(solution)/shard_map/broadcast_in_dim | solution.py:20
  17.8 1.1 fusion.14
  18.9 0.1 broadcast_compare_fusion
  19.2 2.3 %copy.59 = bf16[512,1024]{0,1:T(8,128)(2,1)} copy(bf16[512,1024]{1,0:T(8,128)(2,1)} %param.14) | data formatting | bytes 2097152 | tf_op jit(solution)/shard_map/reshape | solution.py:83
  21.5 4.7 %collective-permute-start.3 = (bf16[128,64]{0,1:T(8,128)(2,1)S(1)}, bf16[128,64]{0,1:T(8,128)(2,1)S(1)}, u32[]{:S(2)}, u32[]{:S(2)}) collective-permute-start(bf16[128,64]{0,1:T(8,128)(2,1)S(1)} %collective-permute-done.1), channel_id=1, source_target_pairs={{4,0},{8,4},{12,8},{16,12},{20,16},{24,20},{28,24},{0,28},{5,1},{9... | collective-permute-start | bytes 49160 | tf_op jit(solution)/shard_map/ppermute | solution.py:30
  26.2 1.1 fusion.13
  27.3 1.1 fusion.12
  28.4 4.7 %collective-permute-start.5 = (bf16[128,64]{0,1:T(8,128)(2,1)S(1)}, bf16[128,64]{0,1:T(8,128)(2,1)S(1)}, u32[]{:S(2)}, u32[]{:S(2)}) collective-permute-start(bf16[128,64]{0,1:T(8,128)(2,1)S(1)} %collective-permute-done.3), channel_id=1, source_target_pairs={{4,0},{8,4},{12,8},{16,12},{20,16},{24,20},{28,24},{0,28},{5,1},{9... | collective-permute-start | bytes 49160 | tf_op jit(solution)/shard_map/ppermute | solution.py:30
  33.1 1.1 fusion.11
  34.3 1.1 fusion.10
  35.4 1.1 fusion.9
  36.5 1.1 fusion.8
  37.6 4.4 %collective-permute-done.6 = bf16[128,64]{0,1:T(8,128)(2,1)S(1)} collective-permute-done((bf16[128,64]{0,1:T(8,128)(2,1)S(1)}, bf16[128,64]{0,1:T(8,128)(2,1)S(1)}, u32[]{:S(2)}, u32[]{:S(2)}) %collective-permute-start.6) | collective-permute-done | bytes 16416 | tf_op jit(solution)/shard_map/ppermute | solution.py:30
  42.0 1.1 fusion.7
  43.1 9.6 %all-gather.3.cloned.1.call-done = bf16[1024,512]{1,0:T(8,128)(2,1)} async-done(((bf16[128,512]{1,0:T(8,128)(2,1)}), bf16[1024,512]{1,0:T(8,128)(2,1)}) %all-gather.3.cloned.1.call-update) | async-done | bytes 1048592 | tf_op jit(solution)/shard_map/all_gather | solution.py:57
  52.8 6.3 %select_reduce_fusion = (f32[8,128]{1,0:T(8,128)S(1)}, f32[8,128,1024]{2,1,0:T(8,128)}) fusion(pred[128,1024]{1,0:T(8,128)(4,1)S(1)} %broadcast_compare_fusion, f32[8,128,1024]{2,1,0:T(8,128)} %fusion.7, bf16[1024,512]{1,0:T(8,128)(2,1)} %all-gather.3.cloned.1.call-done, bf16[512,1024]{1,0:T(8,128)(2,1)S(1)} %copy-done.1, bf16[128,1024]{1,0:T(8,128)(2,1)S(1)} %copy-done.3), kind=kOutput, calls=%fused_computation.1 | convolution fusion | flops 1212677120 | bytes 10883072 | tf_op jit(solution)/shard_map/htl,kl->htk/dot_general | solution.py:62
  59.1 3.3 %fusion = f32[8,128]{1,0:T(8,128)S(1)} fusion(f32[8,128,1024]{2,1,0:T(8,128)} %get-tuple-element.6, f32[8,128]{1,0:T(8,128)S(1)} %broadcast_maximum_fusion, pred[128,1024]{1,0:T(8,128)(4,1)S(1)} %broadcast_compare_fusion), kind=kLoop, calls=%fused_computation.3 | loop fusion | flops 3144704 | bytes 4333568 | tf_op jit(solution)/shard_map/reduce_sum | solution.py:76
  62.4 4.8 %convolution_convert_fusion.2 = bf16[8,128,128]{1,2,0:T(8,128)(2,1)} fusion(bf16[512,8,128]{0,2,1:T(8,128)(2,1)} %bitcast.120, f32[8,128]{1,0:T(8,128)S(1)} %fusion, f32[8,128,1024]{2,1,0:T(8,128)} %get-tuple-element.6, f32[8,128]{1,0:T(8,128)S(1)} %broadcast_maximum_fusion, pred[128,1024]{1,0:T(8,128)(4,1)S(1)} %broadcast_compare_fusion, ...), kind=kOutput, calls=%fused_computation.28 | convolution fusion | flops 1212284928 | bytes 6692864 | tf_op jit(solution)/shard_map/htl,lhv->thv/dot_general | solution.py:82
  67.2 0.0 all-gather.5.cloned.1.call-update
  67.2 0.0 reduce-scatter.2.cloned.1.call-start
  67.2 49.0 %all-gather.5.cloned.1.call-done = bf16[1024,1024]{0,1:T(8,128)(2,1)} async-done(((bf16[128,1024]{0,1:T(8,128)(2,1)}), bf16[1024,1024]{0,1:T(8,128)(2,1)}) %all-gather.5.cloned.1.call-update) | async-done | bytes 2097168 | tf_op jit(solution)/shard_map/all_gather | solution.py:87
  116.3 4.0 %convolution_convert_fusion = bf16[1024,896]{1,0:T(8,128)(2,1)S(1)} fusion(bf16[1024,1024]{0,1:T(8,128)(2,1)} %all-gather.5.cloned.1.call-done, bf16[1024,896]{1,0:T(8,128)(2,1)S(1)} %copy-done), kind=kOutput, calls=%fused_computation.10 | convolution fusion | flops 1879965696 | bytes 5767168 | tf_op jit(solution)/shard_map/dot_general | solution.py:86
  120.2 45.3 %all_to_all.19 = bf16[8,128,896]{2,1,0:T(8,128)(2,1)S(1)} all-to-all(bf16[8,128,896]{2,1,0:T(8,128)(2,1)S(1)} %bitcast.119), channel_id=1, replica_groups=mesh['ctx'=8,'head'=4] {'ctx'}, dimensions={0} | all-to-all | bytes 3670016 | tf_op jit(solution)/shard_map/all_to_all | solution.py:91
  165.5 1.5 copy.62
  167.0 28.8 %reduce-scatter.2.cloned.1.call-done = bf16[128,1792]{1,0:T(8,128)(2,1)} async-done(((bf16[128,7168]{1,0:T(8,128)(2,1)}), bf16[128,1792]{1,0:T(8,128)(2,1)}) %reduce-scatter.2.cloned.1.call-update) | async-done | bytes 458768 | tf_op jit(solution)/shard_map/reduce_scatter | solution.py:93
  (26 shorter events, 0.1 us)
Async XLA Ops:
  6.5 109.7 %copy-start = (bf16[1024,896]{1,0:T(8,128)(2,1)S(1)}, bf16[1024,896]{1,0:T(8,128)(2,1)}, u32[]{:S(2)}) copy-start(bf16[1024,896]{1,0:T(8,128)(2,1)} %param.15) | copy-start | bytes 5505028
  6.5 11.2 %copy-start.4 = (bf16[128,64]{0,1:T(8,128)(2,1)S(1)}, bf16[128,64]{0,1:T(8,128)(2,1)}, u32[]{:S(2)}) copy-start(bf16[128,64]{0,1:T(8,128)(2,1)} %param.11) | copy-start | bytes 49156
  6.5 46.2 %all-gather.3.cloned.1.call-start = ((), (), s32[]{:S(2)}) async-start(), calls=%async_computation.2 | async-start | bytes 1179648 | tf_op jit(solution)/shard_map/all_gather | solution.py:57
  6.5 14.9 %collective-permute-start = (bf16[128,64]{0,1:T(8,128)(2,1)}, bf16[128,64]{0,1:T(8,128)(2,1)S(1)}, u32[]{:S(2)}, u32[]{:S(2)}) collective-permute-start(bf16[128,64]{0,1:T(8,128)(2,1)} %param.11), channel_id=1, source_target_pairs={{0,4},{4,8},{8,12},{12,16},{16,20},{20,24},{24,28},{28,0},{1,5},{5... | collective-permute-start | bytes 49160 | tf_op jit(solution)/shard_map/ppermute | solution.py:17
  9.5 11.9 %collective-permute-start.1 = (bf16[128,64]{0,1:T(8,128)(2,1)}, bf16[128,64]{0,1:T(8,128)(2,1)S(1)}, u32[]{:S(2)}, u32[]{:S(2)}) collective-permute-start(bf16[128,64]{0,1:T(8,128)(2,1)} %param.11), channel_id=1, source_target_pairs={{4,0},{8,4},{12,8},{16,12},{20,16},{24,20},{28,24},{0,28},{5,1},{9... | collective-permute-start | bytes 49160 | tf_op jit(solution)/shard_map/ppermute | solution.py:17
  12.6 103.6 %all-gather.5.cloned.1.call-start = ((), (), s32[]{:S(2)}) async-start(), calls=%async_computation.3 | async-start | bytes 2359296 | tf_op jit(solution)/shard_map/all_gather | solution.py:87
  17.8 35.0 %copy-start.1 = (bf16[512,1024]{1,0:T(8,128)(2,1)S(1)}, bf16[512,1024]{1,0:T(8,128)(2,1)}, u32[]{:S(2)}) copy-start(bf16[512,1024]{1,0:T(8,128)(2,1)} %param.13) | copy-start | bytes 3145732
  17.8 35.0 %copy-start.3 = (bf16[128,1024]{1,0:T(8,128)(2,1)S(1)}, bf16[128,1024]{1,0:T(8,128)(2,1)}, u32[]{:S(2)}) copy-start(bf16[128,1024]{1,0:T(8,128)(2,1)} %param.8) | copy-start | bytes 786436
  21.4 7.0 %collective-permute-start.2 = (bf16[128,64]{0,1:T(8,128)(2,1)S(1)}, bf16[128,64]{0,1:T(8,128)(2,1)S(1)}, u32[]{:S(2)}, u32[]{:S(2)}) collective-permute-start(bf16[128,64]{0,1:T(8,128)(2,1)S(1)} %collective-permute-done), channel_id=1, source_target_pairs={{0,4},{4,8},{8,12},{12,16},{16,20},{20,24},{24,28},{28,0},{1,5},{5... | collective-permute-start | bytes 49160 | tf_op jit(solution)/shard_map/ppermute | solution.py:30
  21.5 7.0 %collective-permute-start.3 = (bf16[128,64]{0,1:T(8,128)(2,1)S(1)}, bf16[128,64]{0,1:T(8,128)(2,1)S(1)}, u32[]{:S(2)}, u32[]{:S(2)}) collective-permute-start(bf16[128,64]{0,1:T(8,128)(2,1)S(1)} %collective-permute-done.1), channel_id=1, source_target_pairs={{4,0},{8,4},{12,8},{16,12},{20,16},{24,20},{28,24},{0,28},{5,1},{9... | collective-permute-start | bytes 49160 | tf_op jit(solution)/shard_map/ppermute | solution.py:30
  28.4 7.0 %collective-permute-start.4 = (bf16[128,64]{0,1:T(8,128)(2,1)S(1)}, bf16[128,64]{0,1:T(8,128)(2,1)S(1)}, u32[]{:S(2)}, u32[]{:S(2)}) collective-permute-start(bf16[128,64]{0,1:T(8,128)(2,1)S(1)} %collective-permute-done.2), channel_id=1, source_target_pairs={{0,4},{4,8},{8,12},{12,16},{16,20},{20,24},{24,28},{28,0},{1,5},{5... | collective-permute-start | bytes 49160 | tf_op jit(solution)/shard_map/ppermute | solution.py:30
  28.4 8.1 %collective-permute-start.5 = (bf16[128,64]{0,1:T(8,128)(2,1)S(1)}, bf16[128,64]{0,1:T(8,128)(2,1)S(1)}, u32[]{:S(2)}, u32[]{:S(2)}) collective-permute-start(bf16[128,64]{0,1:T(8,128)(2,1)S(1)} %collective-permute-done.3), channel_id=1, source_target_pairs={{4,0},{8,4},{12,8},{16,12},{20,16},{24,20},{28,24},{0,28},{5,1},{9... | collective-permute-start | bytes 49160 | tf_op jit(solution)/shard_map/ppermute | solution.py:30
  35.4 6.6 %collective-permute-start.6 = (bf16[128,64]{0,1:T(8,128)(2,1)S(1)}, bf16[128,64]{0,1:T(8,128)(2,1)S(1)}, u32[]{:S(2)}, u32[]{:S(2)}) collective-permute-start(bf16[128,64]{0,1:T(8,128)(2,1)S(1)} %collective-permute-done.4), channel_id=1, source_target_pairs={{0,4},{4,8},{8,12},{12,16},{16,20},{20,24},{24,28},{28,0},{1,5},{5... | collective-permute-start | bytes 49160 | tf_op jit(solution)/shard_map/ppermute | solution.py:30
  59.1 3.3 %copy-start.2 = (bf16[1024,512]{1,0:T(8,128)(2,1)S(1)}, bf16[1024,512]{1,0:T(8,128)(2,1)}, u32[]{:S(2)}) copy-start(bf16[1024,512]{1,0:T(8,128)(2,1)} %all-gather.3.cloned.1.call-done) | copy-start | bytes 3145732
  67.2 128.6 %reduce-scatter.2.cloned.1.call-start = ((), (), s32[]{:S(2)}) async-start(), calls=%async_computation.4 | async-start | bytes 2293760 | tf_op jit(solution)/shard_map/reduce_scatter | solution.py:93
Sparse Core Ops, SparseCore 0:
  12.8 39.9 all-gather.2
  67.3 48.9 all-gather.4
  167.2 28.5 reduce-scatter.1
